TPU v7x, 128 devices: a whole 4x4x4 slice. The times are simulated.
128 devices in a mesh: gx: 16 (over x, z), gy: 8 (over y, core).
Axes of the slice: x: 4, y: 4, z: 4, core: 2. Of those that a mesh axis runs over, the one named last changes fastest.
Arguments:
- velocity: float32 [3, 512, 512, 128], P(None, 'gx', 'gy'), may hold values from -6 to 6
- forces: float32 [16384, 3, 256], P(('gx', 'gy')), may hold values from -48 to 48
- offsets: float32 [16384, 3, 256], P(('gx', 'gy')), may hold values from 0 to 1
- base_x: int32 [16384, 256], P(('gx', 'gy')), may hold values from 0 to 12
- base_y: int32 [16384, 256], P(('gx', 'gy')), may hold values from 0 to 4
- base_z: int32 [16384, 256], P(('gx', 'gy')), may hold values from 0 to 124
- home_device: int32 [16384, 1], P(('gx', 'gy')), may hold values from 0 to 127; in each aligned block of 128 rows (0 to 127, 128 to 255, ...) at most 2 rows name the same one
- home_tile: int32 [16384], P(('gx', 'gy')), may hold values from 0 to 15
Outputs:
- velocity_next: float32 [3, 512, 512, 128], P(None, 'gx', 'gy')
- fibre_velocity: float32 [16384, 3, 256], P(('gx', 'gy'))
Inputs may be any that keep to these rules, and one draw needn't show every extreme that they name: `home_device`: among the 128 blocks of one device no home device is named more than 2 times, and in every draw some device names some home exactly 2 times.
All inputs are finite; a program needn't handle non-finite values.
Results may differ from a plain program's by a relative error of at most 0.0035.
Values sent between devices are 32-bit elements; how exact they have to be, the bound alone decides.
No kernel may reach another device: no remote copies, remote signals or barrier semaphores. Data moves between devices by JAX's collectives and lax.ppermute only.
A program may use at most 64 MiB of HBM per device.

v0:
```python
import jax
import jax.numpy as jnp
from jax import lax
from jax.sharding import PartitionSpec as P

TX = 16
TY = 8


time_step = 0.4
viscosity = 0.15


def with_halo(array, sides, width):
    for axis, dim in sides:
        count, length = (lax.axis_size(axis), array.shape[dim])
        up = [(i, (i + 1) % count) for i in range(count - 1)]
        down = [(j, i) for i, j in up]
        last = lax.slice_in_dim(array, length - width, length, axis=dim)
        first = lax.slice_in_dim(array, 0, width, axis=dim)
        before = lax.ppermute(last, axis, up)
        after = lax.ppermute(first, axis, down)
        array = jnp.concatenate([before, array, after], axis=dim)
    return array


def peskin_weights(offset):
    radical = jnp.sqrt(1.0 + 4.0 * offset - 4.0 * offset * offset)
    return (
        (3.0 - 2.0 * offset - radical) / 8.0,
        (3.0 - 2.0 * offset + radical) / 8.0,
        (1.0 + 2.0 * offset + radical) / 8.0,
        (1.0 + 2.0 * offset - radical) / 8.0,
    )


def dense_factor(corner, offset, length):
    cell_ids = jnp.arange(length, dtype=jnp.int32)
    running = jnp.zeros(offset.shape + (length,), offset.dtype)
    for shift_amount, weight in enumerate(peskin_weights(offset)):
        running = running + jnp.where(
            cell_ids == corner[..., None] + shift_amount, weight[..., None], 0.0
        )
    return running


def block_factors(floats_g, index_g, depth_cells):
    along_x = dense_factor(index_g[:, 0], floats_g[:, 3], TX)
    along_y = dense_factor(index_g[:, 1], floats_g[:, 4], TY)
    along_z = dense_factor(index_g[:, 2], floats_g[:, 5], depth_cells)
    group_size, points = (along_x.shape[0], along_x.shape[1])
    kernel_xy = (
        (along_x[:, :, :, None] * along_y[:, :, None, :])
        .reshape(group_size, points, TX * TY)
        .astype(jnp.bfloat16)
    )
    return (kernel_xy, along_z)


def tiles_to_field(tile_data, count_x, count_y, depth_cells):
    shaped = tile_data.reshape(count_x, count_y, TX, TY, 3, depth_cells)
    return jnp.transpose(shaped, (4, 0, 2, 1, 3, 5)).reshape(
        3, count_x * TX, count_y * TY, depth_cells
    )


def field_to_tiles(field, count_x, count_y):
    depth_cells = field.shape[3]
    shaped = field.reshape(3, count_x, TX, count_y, TY, depth_cells)
    return jnp.transpose(shaped, (1, 3, 2, 4, 0, 5)).reshape(
        count_x * count_y, TX * TY, 3 * depth_cells
    )


def fluid_sweep(padded):
    boxed = jnp.pad(padded, ((0, 0), (0, 0), (0, 0), (1, 1)))
    centre = boxed[:, 1:-1, 1:-1, 1:-1]
    plus_x = boxed[:, 2:, 1:-1, 1:-1]
    minus_x = boxed[:, :-2, 1:-1, 1:-1]
    plus_y = boxed[:, 1:-1, 2:, 1:-1]
    minus_y = boxed[:, 1:-1, :-2, 1:-1]
    plus_z = boxed[:, 1:-1, 1:-1, 2:]
    minus_z = boxed[:, 1:-1, 1:-1, :-2]
    laplace = plus_x + minus_x + plus_y + minus_y + plus_z + minus_z - 6.0 * centre
    advect = (
        centre[0:1] * (plus_x - minus_x)
        + centre[1:2] * (plus_y - minus_y)
        + centre[2:3] * (plus_z - minus_z)
    ) * 0.5
    return centre + time_step * (viscosity * laplace - advect)


def body(velocity, forces, offsets, base_x, base_y, base_z, home_device, home_tile):
    count_x = lax.axis_size("gx")
    count_y = lax.axis_size("gy")
    devices_all = count_x * count_y
    blocks, _, points = forces.shape
    capacity = max(2, 2 * blocks // devices_all)
    slot_count = devices_all * capacity
    depth_cells = velocity.shape[3]
    tiles_x = velocity.shape[1] // TX
    tiles_y = velocity.shape[2] // TY
    tile_total = tiles_x * tiles_y
    group_size = 16
    group_count = slot_count // group_size
    target = home_device[:, 0]
    member = (target[:, None] == jnp.arange(devices_all, dtype=jnp.int32)[None, :]).astype(
        jnp.int32
    )
    before = jnp.cumsum(member, axis=0) - member
    slot_rank = jnp.sum(before * member, axis=1)
    slot_index = target * capacity + slot_rank
    payload = jnp.concatenate([forces, offsets], axis=1)
    indices = jnp.stack([base_x, base_y, base_z], axis=1)
    send_float = jnp.zeros((slot_count, 6, points), jnp.float32).at[slot_index].set(payload)
    send_index = jnp.zeros((slot_count, 3, points), jnp.int32).at[slot_index].set(indices)
    send_tile = jnp.full((slot_count,), -1, jnp.int32).at[slot_index].set(home_tile)
    recv_float, recv_index, recv_tile = (
        lax.all_to_all(send_float, ("gx", "gy"), split_axis=0, concat_axis=0, tiled=True),
        lax.all_to_all(send_index, ("gx", "gy"), split_axis=0, concat_axis=0, tiled=True),
        lax.all_to_all(send_tile, ("gx", "gy"), split_axis=0, concat_axis=0, tiled=True),
    )
    group_items = (
        recv_float.reshape(group_count, group_size, 6, points),
        recv_index.reshape(group_count, group_size, 3, points),
        recv_tile.reshape(group_count, group_size),
    )
    tile_ids = jnp.arange(tile_total, dtype=jnp.int32)

    def spread_group(running, items_now):
        floats_g, index_g, tile_g = items_now
        kernel_xy, along_z = block_factors(floats_g, index_g, depth_cells)
        weighted = (
            jnp.transpose(floats_g[:, 0:3], (0, 2, 1))[:, :, :, None] * along_z[:, :, None, :]
        )
        weighted = weighted.reshape(group_size, points, 3 * depth_cells).astype(jnp.bfloat16)
        pieces = jnp.einsum("gpa,gpb->gab", kernel_xy, weighted, preferred_element_type=jnp.float32)
        select = (tile_g[:, None] == tile_ids[None, :]).astype(jnp.float32)
        return (
            running + jnp.einsum("gt,gab->tab", select, pieces, precision=lax.Precision.HIGHEST),
            None,
        )

    start = jnp.zeros((tile_total, TX * TY, 3 * depth_cells), jnp.float32)
    force_tiles, _ = lax.scan(spread_group, start, group_items)
    force_field = tiles_to_field(force_tiles, tiles_x, tiles_y, depth_cells)
    forced = velocity + time_step * force_field
    padded = with_halo(forced, (("gx", 1), ("gy", 2)), 1)
    velocity_next = fluid_sweep(padded)
    tiled = field_to_tiles(velocity_next, tiles_x, tiles_y).astype(jnp.bfloat16)

    def interpolate_group(carry, items_now):
        floats_g, index_g, tile_g = items_now
        kernel_xy, along_z = block_factors(floats_g, index_g, depth_cells)
        fetched = tiled[jnp.clip(tile_g, 0, tile_total - 1)]
        hidden = jnp.einsum("gpa,gab->gpb", kernel_xy, fetched, preferred_element_type=jnp.float32)
        hidden = hidden.reshape(group_size, points, 3, depth_cells)
        result = jnp.sum(hidden * along_z[:, :, None, :], axis=3)
        return (carry, jnp.transpose(result, (0, 2, 1)))

    _, replies = lax.scan(interpolate_group, jnp.zeros((), jnp.float32), group_items)
    replies = replies.reshape(slot_count, 3, points)
    returned = lax.all_to_all(replies, ("gx", "gy"), split_axis=0, concat_axis=0, tiled=True)
    fibre_velocity = returned[slot_index]
    return (velocity_next, fibre_velocity)


def solution(mesh):
    return jax.shard_map(
        body,
        mesh=mesh,
        in_specs=(
            P(None, "gx", "gy", None),
            P(("gx", "gy"), None, None),
            P(("gx", "gy"), None, None),
            P(("gx", "gy"), None),
            P(("gx", "gy"), None),
            P(("gx", "gy"), None),
            P(("gx", "gy"), None),
            P(("gx", "gy")),
        ),
        out_specs=(P(None, "gx", "gy", None), P(("gx", "gy"), None, None)),
        check_vma=False,
    )
```

profile of v0, /device:TPU:1, one launch (start us, length us, event | category | flops | bytes accessed | tf_op | source)
XLA Modules:
  0.0 515.0 jit_solution(11184300293678976367)
XLA Ops:
  4.9 11.5 %all-to-all-start = ((s32[128,2,1]{1,2,0:T(1,128)}), s32[128,2,1]{1,2,0:T(1,128)S(1)}, u32[]{:S(2)}, u32[]{:S(2)}) async-start(s32[128,2,1]{1,2,0:T(1,128)} %bitcast.17), calls=%async_computation | async-start | bytes 131072 | tf_op jit(solution)/shard_map/all_to_all | solution.py:121
  19.0 13.2 %scatter_fusion = s32[256,3,256]{2,1,0:T(4,128)} fusion(s32[256,3,256]{2,1,0:T(4,128)} %broadcast_in_dim.252, s32[128]{0:T(128)S(1)} %fusion.43, s32[128,3,256]{2,1,0:T(4,128)S(1)} %copy.35), kind=kCustom, calls=%fused_computation.3 | custom fusion | bytes 1180160 | tf_op jit(solution)/shard_map/scatter | solution.py:116
  32.1 9.8 %all-to-all-start.1 = ((s32[256,3,256]{2,1,0:T(4,128)}), s32[256,3,256]{2,1,0:T(4,128)S(1)}, u32[]{:S(2)}, u32[]{:S(2)}) async-start(s32[256,3,256]{2,1,0:T(4,128)} %scatter_fusion), calls=%async_computation.1 | async-start | bytes 2097152 | tf_op jit(solution)/shard_map/all_to_all | solution.py:120
  42.5 1.5 broadcast_in_dim.253
  44.0 13.7 %scatter_fusion.1 = f32[256,6,256]{2,1,0:T(8,128)} fusion(f32[256,6,256]{2,1,0:T(8,128)} %broadcast_in_dim.253, s32[128]{0:T(128)S(1)} %fusion.43, f32[128,6,256]{2,1,0:T(8,128)S(1)} %copy.36), kind=kCustom, calls=%fused_computation.4 | custom fusion | bytes 2359808 | tf_op jit(solution)/shard_map/scatter | solution.py:115
  57.7 3.3 all-to-all-done.1
  60.9 6.5 %all-to-all-start.2 = ((f32[256,6,256]{2,1,0:T(8,128)}), f32[256,6,256]{2,1,0:T(8,128)S(1)}, u32[]{:S(2)}, u32[]{:S(2)}) async-start(f32[256,6,256]{2,1,0:T(8,128)} %scatter_fusion.1), calls=%async_computation.2 | async-start | bytes 4194304 | tf_op jit(solution)/shard_map/all_to_all | solution.py:119
  70.0 27.6 %all-to-all-done.2 = f32[256,6,256]{2,1,0:T(8,128)S(1)} async-done(((f32[256,6,256]{2,1,0:T(8,128)}), f32[256,6,256]{2,1,0:T(8,128)S(1)}, u32[]{:S(2)}, u32[]{:S(2)}) %all-to-all-start.2) | async-done | bytes 1572896 | tf_op jit(solution)/shard_map/all_to_all | solution.py:119
  97.6 1.7 copy.38
  99.3 198.4 %while.22 = (s32[]{:T(128)}, f32[16,128,384]{2,0,1:T(8,128)}, s32[16,16]{1,0:T(8,128)S(1)}, s32[16,16,3,256]{3,1,2,0:T(8,128)}, f32[16,16,6,256]{3,1,2,0:T(8,128)}, /*index=5*/s32[]{:T(128)}, s32[]{:T(128)}) while((s32[]{:T(128)}, f32[16,128,384]{2,0,1:T(8,128)}, s32[16,16]{1,0:T(8,128)S(1)}, s32[16,16,3,256]{3,1,2,0:T(8,128)}, ...), condition=%wide.region_6.7_spmd.clone, body=%wide.region_5.6_spmd.clone.sunk | while | flops 566485248 | bytes 25329956 | solution.py:145
  101.1 1.4 select_add_fusion.17
  104.8 5.2 %select_add_fusion.20 = f32[16,128,384]{2,0,1:T(8,128)} fusion(f32[16,128,384]{2,0,1:T(8,128)} %get-tuple-element.371, f32[16,128,384]{2,1,0:T(8,128)S(1)} %fusion.68, pred[]{:T(512)S(6)} %compare.22, s32[16]{0:T(128)S(1)} %fusion.69), kind=kOutput, calls=%fused_computation.81.clone.1 | convolution fusion | flops 152568064 | bytes 9437249 | tf_op jit(solution)/shard_map/while/body/eval_jaxpr/gt,gab->tab/dot_general | solution.py:140
  111.7 1.4 select_add_fusion.17
  115.4 7.1 %select_add_fusion.20 = f32[16,128,384]{2,0,1:T(8,128)} fusion(f32[16,128,384]{2,0,1:T(8,128)} %get-tuple-element.371, f32[16,128,384]{2,1,0:T(8,128)S(1)} %fusion.68, pred[]{:T(512)S(6)} %compare.22, s32[16]{0:T(128)S(1)} %fusion.69), kind=kOutput, calls=%fused_computation.81.clone.1 | convolution fusion | flops 152568064 | bytes 9437249 | tf_op jit(solution)/shard_map/while/body/eval_jaxpr/gt,gab->tab/dot_general | solution.py:140
  124.3 1.4 select_add_fusion.17
  127.9 7.1 %select_add_fusion.20 = f32[16,128,384]{2,0,1:T(8,128)} fusion(f32[16,128,384]{2,0,1:T(8,128)} %get-tuple-element.371, f32[16,128,384]{2,1,0:T(8,128)S(1)} %fusion.68, pred[]{:T(512)S(6)} %compare.22, s32[16]{0:T(128)S(1)} %fusion.69), kind=kOutput, calls=%fused_computation.81.clone.1 | convolution fusion | flops 152568064 | bytes 9437249 | tf_op jit(solution)/shard_map/while/body/eval_jaxpr/gt,gab->tab/dot_general | solution.py:140
  136.8 1.4 select_add_fusion.17
  140.5 7.1 %select_add_fusion.20 = f32[16,128,384]{2,0,1:T(8,128)} fusion(f32[16,128,384]{2,0,1:T(8,128)} %get-tuple-element.371, f32[16,128,384]{2,1,0:T(8,128)S(1)} %fusion.68, pred[]{:T(512)S(6)} %compare.22, s32[16]{0:T(128)S(1)} %fusion.69), kind=kOutput, calls=%fused_computation.81.clone.1 | convolution fusion | flops 152568064 | bytes 9437249 | tf_op jit(solution)/shard_map/while/body/eval_jaxpr/gt,gab->tab/dot_general | solution.py:140
  149.3 1.4 select_add_fusion.17
  153.0 7.1 %select_add_fusion.20 = f32[16,128,384]{2,0,1:T(8,128)} fusion(f32[16,128,384]{2,0,1:T(8,128)} %get-tuple-element.371, f32[16,128,384]{2,1,0:T(8,128)S(1)} %fusion.68, pred[]{:T(512)S(6)} %compare.22, s32[16]{0:T(128)S(1)} %fusion.69), kind=kOutput, calls=%fused_computation.81.clone.1 | convolution fusion | flops 152568064 | bytes 9437249 | tf_op jit(solution)/shard_map/while/body/eval_jaxpr/gt,gab->tab/dot_general | solution.py:140
  161.8 1.4 select_add_fusion.17
  165.5 7.1 %select_add_fusion.20 = f32[16,128,384]{2,0,1:T(8,128)} fusion(f32[16,128,384]{2,0,1:T(8,128)} %get-tuple-element.371, f32[16,128,384]{2,1,0:T(8,128)S(1)} %fusion.68, pred[]{:T(512)S(6)} %compare.22, s32[16]{0:T(128)S(1)} %fusion.69), kind=kOutput, calls=%fused_computation.81.clone.1 | convolution fusion | flops 152568064 | bytes 9437249 | tf_op jit(solution)/shard_map/while/body/eval_jaxpr/gt,gab->tab/dot_general | solution.py:140
  178.0 7.1 %select_add_fusion.20 = f32[16,128,384]{2,0,1:T(8,128)} fusion(f32[16,128,384]{2,0,1:T(8,128)} %get-tuple-element.371, f32[16,128,384]{2,1,0:T(8,128)S(1)} %fusion.68, pred[]{:T(512)S(6)} %compare.22, s32[16]{0:T(128)S(1)} %fusion.69), kind=kOutput, calls=%fused_computation.81.clone.1 | convolution fusion | flops 152568064 | bytes 9437249 | tf_op jit(solution)/shard_map/while/body/eval_jaxpr/gt,gab->tab/dot_general | solution.py:140
  190.5 7.1 %select_add_fusion.20 = f32[16,128,384]{2,0,1:T(8,128)} fusion(f32[16,128,384]{2,0,1:T(8,128)} %get-tuple-element.371, f32[16,128,384]{2,1,0:T(8,128)S(1)} %fusion.68, pred[]{:T(512)S(6)} %compare.22, s32[16]{0:T(128)S(1)} %fusion.69), kind=kOutput, calls=%fused_computation.81.clone.1 | convolution fusion | flops 152568064 | bytes 9437249 | tf_op jit(solution)/shard_map/while/body/eval_jaxpr/gt,gab->tab/dot_general | solution.py:140
  199.4 1.4 select_add_fusion.17
  203.0 7.1 %select_add_fusion.20 = f32[16,128,384]{2,0,1:T(8,128)} fusion(f32[16,128,384]{2,0,1:T(8,128)} %get-tuple-element.371, f32[16,128,384]{2,1,0:T(8,128)S(1)} %fusion.68, pred[]{:T(512)S(6)} %compare.22, s32[16]{0:T(128)S(1)} %fusion.69), kind=kOutput, calls=%fused_computation.81.clone.1 | convolution fusion | flops 152568064 | bytes 9437249 | tf_op jit(solution)/shard_map/while/body/eval_jaxpr/gt,gab->tab/dot_general | solution.py:140
  211.9 1.4 select_add_fusion.17
  215.6 7.1 %select_add_fusion.20 = f32[16,128,384]{2,0,1:T(8,128)} fusion(f32[16,128,384]{2,0,1:T(8,128)} %get-tuple-element.371, f32[16,128,384]{2,1,0:T(8,128)S(1)} %fusion.68, pred[]{:T(512)S(6)} %compare.22, s32[16]{0:T(128)S(1)} %fusion.69), kind=kOutput, calls=%fused_computation.81.clone.1 | convolution fusion | flops 152568064 | bytes 9437249 | tf_op jit(solution)/shard_map/while/body/eval_jaxpr/gt,gab->tab/dot_general | solution.py:140
  228.1 7.1 %select_add_fusion.20 = f32[16,128,384]{2,0,1:T(8,128)} fusion(f32[16,128,384]{2,0,1:T(8,128)} %get-tuple-element.371, f32[16,128,384]{2,1,0:T(8,128)S(1)} %fusion.68, pred[]{:T(512)S(6)} %compare.22, s32[16]{0:T(128)S(1)} %fusion.69), kind=kOutput, calls=%fused_computation.81.clone.1 | convolution fusion | flops 152568064 | bytes 9437249 | tf_op jit(solution)/shard_map/while/body/eval_jaxpr/gt,gab->tab/dot_general | solution.py:140
  236.9 1.4 select_add_fusion.17
  240.6 7.1 %select_add_fusion.20 = f32[16,128,384]{2,0,1:T(8,128)} fusion(f32[16,128,384]{2,0,1:T(8,128)} %get-tuple-element.371, f32[16,128,384]{2,1,0:T(8,128)S(1)} %fusion.68, pred[]{:T(512)S(6)} %compare.22, s32[16]{0:T(128)S(1)} %fusion.69), kind=kOutput, calls=%fused_computation.81.clone.1 | convolution fusion | flops 152568064 | bytes 9437249 | tf_op jit(solution)/shard_map/while/body/eval_jaxpr/gt,gab->tab/dot_general | solution.py:140
  249.4 1.4 select_add_fusion.17
  253.1 7.1 %select_add_fusion.20 = f32[16,128,384]{2,0,1:T(8,128)} fusion(f32[16,128,384]{2,0,1:T(8,128)} %get-tuple-element.371, f32[16,128,384]{2,1,0:T(8,128)S(1)} %fusion.68, pred[]{:T(512)S(6)} %compare.22, s32[16]{0:T(128)S(1)} %fusion.69), kind=kOutput, calls=%fused_computation.81.clone.1 | convolution fusion | flops 152568064 | bytes 9437249 | tf_op jit(solution)/shard_map/while/body/eval_jaxpr/gt,gab->tab/dot_general | solution.py:140
  262.0 1.4 select_add_fusion.17
  265.6 7.1 %select_add_fusion.20 = f32[16,128,384]{2,0,1:T(8,128)} fusion(f32[16,128,384]{2,0,1:T(8,128)} %get-tuple-element.371, f32[16,128,384]{2,1,0:T(8,128)S(1)} %fusion.68, pred[]{:T(512)S(6)} %compare.22, s32[16]{0:T(128)S(1)} %fusion.69), kind=kOutput, calls=%fused_computation.81.clone.1 | convolution fusion | flops 152568064 | bytes 9437249 | tf_op jit(solution)/shard_map/while/body/eval_jaxpr/gt,gab->tab/dot_general | solution.py:140
  278.1 7.1 %select_add_fusion.20 = f32[16,128,384]{2,0,1:T(8,128)} fusion(f32[16,128,384]{2,0,1:T(8,128)} %get-tuple-element.371, f32[16,128,384]{2,1,0:T(8,128)S(1)} %fusion.68, pred[]{:T(512)S(6)} %compare.22, s32[16]{0:T(128)S(1)} %fusion.69), kind=kOutput, calls=%fused_computation.81.clone.1 | convolution fusion | flops 152568064 | bytes 9437249 | tf_op jit(solution)/shard_map/while/body/eval_jaxpr/gt,gab->tab/dot_general | solution.py:140
  287.0 1.4 select_add_fusion.17
  290.7 7.1 %select_add_fusion.20 = f32[16,128,384]{2,0,1:T(8,128)} fusion(f32[16,128,384]{2,0,1:T(8,128)} %get-tuple-element.371, f32[16,128,384]{2,1,0:T(8,128)S(1)} %fusion.68, pred[]{:T(512)S(6)} %compare.22, s32[16]{0:T(128)S(1)} %fusion.69), kind=kOutput, calls=%fused_computation.81.clone.1 | convolution fusion | flops 152568064 | bytes 9437249 | tf_op jit(solution)/shard_map/while/body/eval_jaxpr/gt,gab->tab/dot_general | solution.py:140
  297.7 2.2 broadcast_multiply_fusion
  303.8 4.0 collective-permute-start.1
  307.8 1.6 collective-permute-done.1
  309.5 4.3 collective-permute-start.2
  313.8 2.1 collective-permute-start.3
  316.9 4.5 select_maximum_fusion
  321.4 7.3 %fusion.46 = (bf16[3,32,64,128]{3,2,1,0:T(8,128)(2,1)S(1)}, f32[3,32,64,128]{3,2,1,0:T(8,128)}) fusion(f32[3,32,64,128]{3,2,1,0:T(8,128)S(1)} %add.577, f32[32,64,128]{2,1,0:T(8,128)S(1)} %get-tuple-element.197, f32[32,64,128]{2,1,0:T(8,128)S(1)} %get-tuple-element.198, f32[32,64,128]{2,1,0:T(8,128)S(1)} %get-tuple-element.196, ...), kind=kLoop, calls=%fused_computation.186 | loop fusion | flops 22806528 | bytes 17602560 | tf_op jit(solution)/shard_map/convert_element_type | solution.py:150
  329.0 156.2 %while.21 = (s32[]{:T(128)}, f32[16,16,3,256]{3,2,1,0:T(4,128)}, s32[16,16,3,256]{3,1,2,0:T(8,128)}, f32[16,16,6,256]{3,1,2,0:T(8,128)}, s32[16,16]{1,0:T(8,128)...) while((s32[]{:T(128)}, f32[16,16,3,256]{3,2,1,0:T(4,128)}, s32[16,16,3,256]{3,1,2,0:T(8,128)}, ...), condition=%wide.region_9.10_spmd, body=%wide.region_7.9_spmd.sunk | while | flops 413905984 | bytes 24147028 | solution.py:161
  485.3 9.0 %all-to-all-start.3 = ((f32[256,3,256]{2,1,0:T(4,128)}), f32[256,3,256]{2,1,0:T(4,128)S(1)}, u32[]{:S(2)}, u32[]{:S(2)}) async-start(f32[256,3,256]{2,1,0:T(4,128)} %bitcast.298), calls=%async_computation.3 | async-start | bytes 2097152 | tf_op jit(solution)/shard_map/all_to_all | solution.py:163
  494.9 18.4 %all-to-all-done.3 = f32[256,3,256]{2,1,0:T(4,128)S(1)} async-done(((f32[256,3,256]{2,1,0:T(4,128)}), f32[256,3,256]{2,1,0:T(4,128)S(1)}, u32[]{:S(2)}, u32[]{:S(2)}) %all-to-all-start.3) | async-done | bytes 786464 | tf_op jit(solution)/shard_map/all_to_all | solution.py:163
  (747 shorter events, 240.0 us)
Async XLA Ops:
  3.0 40.9 %copy-start.12 = (s32[128]{0:T(128)}, s32[128]{0:T(128)S(1)}, u32[]{:S(2)}) copy-start(s32[128]{0:T(128)S(1)} %fusion.43) | copy-start | bytes 1540
  4.9 27.2 %all-to-all-start = ((s32[128,2,1]{1,2,0:T(1,128)}), s32[128,2,1]{1,2,0:T(1,128)S(1)}, u32[]{:S(2)}, u32[]{:S(2)}) async-start(s32[128,2,1]{1,2,0:T(1,128)} %bitcast.17), calls=%async_computation | async-start | bytes 131072 | tf_op jit(solution)/shard_map/all_to_all | solution.py:121
  16.4 25.5 %copy-start.8 = (f32[128,3,256]{2,0,1:T(8,128)S(1)}, f32[128,3,256]{2,0,1:T(8,128)}, u32[]{:S(2)}) copy-start(f32[128,3,256]{2,0,1:T(8,128)} %param.14) | copy-start | bytes 1179652
  16.4 25.5 %copy-start.9 = (f32[128,3,256]{2,0,1:T(8,128)S(1)}, f32[128,3,256]{2,0,1:T(8,128)}, u32[]{:S(2)}) copy-start(f32[128,3,256]{2,0,1:T(8,128)} %param.13) | copy-start | bytes 1179652
  32.1 28.8 %all-to-all-start.1 = ((s32[256,3,256]{2,1,0:T(4,128)}), s32[256,3,256]{2,1,0:T(4,128)S(1)}, u32[]{:S(2)}, u32[]{:S(2)}) async-start(s32[256,3,256]{2,1,0:T(4,128)} %scatter_fusion), calls=%async_computation.1 | async-start | bytes 2097152 | tf_op jit(solution)/shard_map/all_to_all | solution.py:120
  60.9 36.7 %all-to-all-start.2 = ((f32[256,6,256]{2,1,0:T(8,128)}), f32[256,6,256]{2,1,0:T(8,128)S(1)}, u32[]{:S(2)}, u32[]{:S(2)}) async-start(f32[256,6,256]{2,1,0:T(8,128)} %scatter_fusion.1), calls=%async_computation.2 | async-start | bytes 4194304 | tf_op jit(solution)/shard_map/all_to_all | solution.py:119
  299.9 1.9 copy-start
  302.5 5.4 %collective-permute-start = (f32[3,1,64,128]{3,2,1,0:T(8,128)S(1)}, f32[3,1,64,128]{3,2,1,0:T(8,128)S(1)}, u32[]{:S(2)}, u32[]{:S(2)}) collective-permute-start(f32[3,1,64,128]{3,2,1,0:T(8,128)S(1)} %get-tuple-element.195), channel_id=1, source_target_pairs={{8,0},{16,8},{24,16},{32,24},{40,32},{48,40},{56,48},{64,56},{72,6... | collective-permute-start | bytes 294920 | tf_op jit(solution)/shard_map/ppermute | solution.py:22
  303.8 5.6 %collective-permute-start.1 = (f32[3,1,64,128]{3,2,1,0:T(8,128)S(1)}, f32[3,1,64,128]{3,2,1,0:T(8,128)S(1)}, u32[]{:S(2)}, u32[]{:S(2)}) collective-permute-start(f32[3,1,64,128]{3,2,1,0:T(8,128)S(1)} %get-tuple-element.194), channel_id=1, source_target_pairs={{0,8},{8,16},{16,24},{24,32},{32,40},{40,48},{48,56},{56,64},{64,7... | collective-permute-start | bytes 294920 | tf_op jit(solution)/shard_map/ppermute | solution.py:21
  309.5 6.9 %collective-permute-start.2 = (f32[3,34,1,128]{3,2,1,0:T(1,128)S(1)}, f32[3,34,1,128]{3,2,1,0:T(1,128)S(1)}, u32[]{:S(2)}, u32[]{:S(2)}) collective-permute-start(f32[3,34,1,128]{3,2,1,0:T(1,128)S(1)} %get-tuple-element.193), channel_id=1, source_target_pairs={{1,0},{2,1},{3,2},{4,3},{5,4},{6,5},{7,6},{9,8},{10,9},{11,10},{12... | collective-permute-start | bytes 156680 | tf_op jit(solution)/shard_map/ppermute | solution.py:22
  313.8 3.1 collective-permute-start.3
  329.1 4.4 copy-start.10
  337.1 1.7 copy-start.11
  338.8 4.4 copy-start.10
  346.9 1.7 copy-start.11
  348.6 4.4 copy-start.10
  356.6 1.7 copy-start.11
  358.4 4.4 copy-start.10
  366.4 1.7 copy-start.11
  368.1 4.4 copy-start.10
  376.2 1.7 copy-start.11
  377.9 4.4 copy-start.10
  385.9 1.7 copy-start.11
  387.6 4.4 copy-start.10
  395.7 1.7 copy-start.11
  397.4 4.4 copy-start.10
  405.5 1.7 copy-start.11
  407.2 4.4 copy-start.10
  415.2 1.7 copy-start.11
  416.9 4.4 copy-start.10
  425.0 1.7 copy-start.11
  426.7 4.4 copy-start.10
  434.8 1.7 copy-start.11
  436.5 4.4 copy-start.10
  441.9 1.1 copy-start.1
  441.9 1.1 copy-start.2
  441.9 1.1 copy-start.3
  441.9 1.1 copy-start.4
  444.5 1.7 copy-start.11
  446.2 4.4 copy-start.10
  454.3 1.7 copy-start.11
  456.0 4.4 copy-start.10
  464.0 1.7 copy-start.11
  465.7 4.4 copy-start.10
  473.8 1.7 copy-start.11
  475.5 4.4 copy-start.10
  483.6 1.7 copy-start.11
  485.3 28.0 %all-to-all-start.3 = ((f32[256,3,256]{2,1,0:T(4,128)}), f32[256,3,256]{2,1,0:T(4,128)S(1)}, u32[]{:S(2)}, u32[]{:S(2)}) async-start(f32[256,3,256]{2,1,0:T(4,128)} %bitcast.298), calls=%async_computation.3 | async-start | bytes 2097152 | tf_op jit(solution)/shard_map/all_to_all | solution.py:163
  (108 other events, 120.1 us)
where the time goes:
time: 520 us; the launch traced here: 515 us
  matrix products  144 us (28%)
  other arithmetic  135 us (26%)
  local copies, waits for them, and re-layouts  132 us (25%)
  waiting for transfers between devices  51.5 us (10%)
  starting transfers between devices  48.5 us (9%)
    dot_general x16, matrix products, spread_group(): jnp.einsum('gt,gab->tab', select, pieces, precision=lax.Precision.HIGHEST)  111 us
    squeeze x64, local copies, waits for them, and re-layouts, body(): force_tiles, _ = lax.scan(spread_group, start, group_items)  54.6 us
    add x96, other arithmetic, dense_factor(): running + jnp.where(cell_ids == corner[..., None] + shift_amount, weight[...  52.7 us
    all_to_all x1, waiting for transfers between devices, body(): lax.all_to_all(send_float, ('gx', 'gy'), split_axis=0, concat_axis=0, til...  27.6 us
    all_to_all x1, waiting for transfers between devices, body(): lax.all_to_all(replies, ('gx', 'gy'), split_axis=0, concat_axis=0, tiled=...  18.4 us
    reduce_sum x16, other arithmetic, interpolate_group(): result = jnp.sum(hidden * along_z[:, :, None, :], axis=3)  17 us
    dot_general x16, matrix products, interpolate_group(): jnp.einsum('gpa,gab->gpb', kernel_xy, fetched, preferred_element_type=jnp...  16.5 us
    gather x16, local copies, waits for them, and re-layouts, interpolate_group(): fetched = tiled[jnp.clip(tile_g, 0, tile_total - 1)]  16.2 us
  transfers between devices with their start and end apart: 8, of which 6 were waited for; matrix products, arithmetic and copies ran while one was open for 7% of the time, Pallas kernels for 0%

commit v1 on v0

v1 whole, which is shorter than its diff:
```python
import jax
import jax.numpy as jnp
from jax import lax
from jax.experimental import pallas as pl
from jax.experimental.pallas import tpu as pltpu
from jax.sharding import PartitionSpec as P

TX = 16
TY = 8
ROWS = 40
AXES = ("gx", "gy")

time_step = 0.4
viscosity = 0.15


def force_row(rank, idx):
    k, odd = idx // 2, idx % 2
    return jnp.where(rank == 0, 16 + idx, (6, 30, 38)[k] + odd)


def pack_kernel(home_ref, tile_ref, forces_ref, offsets_ref, bx_ref, by_ref, bz_ref, send_ref, slot_ref, count_ref):
    blocks = forces_ref.shape[1]
    devices = send_ref.shape[0] // ROWS

    def clear(d, carry):
        count_ref[d] = 0
        send_ref[pl.ds(d * ROWS + 14, 2), :] = jnp.full((2, 128), -1.0, jnp.float32)
        return carry

    lax.fori_loop(0, devices, clear, 0, unroll=8)

    def place(group, carry):
        b0 = pl.multiple_of(group * 8, 8)
        rows, marks = [], []
        for j in range(8):
            home = home_ref[b0 + j]
            rank = count_ref[home]
            count_ref[home] = rank + 1
            slot_ref[b0 + j] = home * 2 + rank
            rows.append((home * ROWS, rank))
            marks.append(tile_ref[b0 + j].astype(jnp.float32))
        for q in range(2):
            lanes = slice(q * 128, (q + 1) * 128)
            for v in range(3):
                idx = q * 3 + v
                off = offsets_ref[v, pl.ds(b0, 8), lanes]
                base = (bx_ref, by_ref, bz_ref)[v][pl.ds(b0, 8), lanes].astype(jnp.float32)
                force = forces_ref[v, pl.ds(b0, 8), lanes]
                for j, (row0, rank) in enumerate(rows):
                    send_ref[pl.ds(row0 + 24 * rank + idx, 1), :] = off[j : j + 1, :]
                    send_ref[pl.ds(row0 + 24 * rank + 8 + idx, 1), :] = base[j : j + 1, :]
                    send_ref[pl.ds(row0 + force_row(rank, idx), 1), :] = force[j : j + 1, :]
        for j, (row0, rank) in enumerate(rows):
            send_ref[pl.ds(row0 + 14 + rank, 1), :] = jnp.full((1, 128), marks[j], jnp.float32)
        return carry

    lax.fori_loop(0, blocks // 8, place, 0)


def pack(home, tile, forces, offsets, bx, by, bz, devices):
    smem = pl.BlockSpec(memory_space=pltpu.SMEM)
    vmem = pl.BlockSpec(memory_space=pltpu.VMEM)
    blocks = home.shape[0]
    return pl.pallas_call(
        pack_kernel,
        out_shape=(
            jax.ShapeDtypeStruct((devices * ROWS, 128), jnp.float32),
            jax.ShapeDtypeStruct((blocks,), jnp.int32),
        ),
        in_specs=[smem, smem, vmem, vmem, vmem, vmem, vmem],
        out_specs=(vmem, smem),
        scratch_shapes=[pltpu.SMEM((devices,), jnp.int32)],
        name="pack",
    )(home, tile, forces, offsets, bx, by, bz)


def list_slots(tile_ref, list_ref, count):
    def step(s, n):
        list_ref[n] = s
        return n + (tile_ref[s] >= 0).astype(jnp.int32)

    total = lax.fori_loop(0, count, step, 0, unroll=8)

    @pl.when(total % 2 == 1)
    def _():
        list_ref[total] = list_ref[total - 1]

    return total


def slot_weights(recv_ref, slot):
    device, rank = slot // 2, slot % 2
    row0 = pl.multiple_of(device * ROWS + 24 * rank, 8)
    off = recv_ref[pl.ds(row0, 8), :]
    base = recv_ref[pl.ds(row0 + 8, 8), :]
    square = 1.0 + 4.0 * off - 4.0 * off * off
    rad = square * lax.rsqrt(square)
    low, high = 3.0 - 2.0 * off, 1.0 + 2.0 * off
    weights = [(low - rad) * 0.125, (low + rad) * 0.125, (high + rad) * 0.125, (high - rad) * 0.125]
    corners = [base, base + 1.0, base + 2.0, base + 3.0]
    return corners, weights


def spread_rows(cell, corners, weights, dtype):
    shape = cell.shape
    out = jnp.zeros(shape, dtype)
    for corner, weight in zip(corners, weights):
        out = jnp.where(cell == corner, weight, out)
    return out


def rows_of(values, row, sublanes, dtype):
    return [jnp.broadcast_to(v[row : row + 1, :], (sublanes, 128)).astype(dtype) for v in values]


def weights_x(corners, weights, q):
    cs, ws = rows_of(corners, q * 3, 8, jnp.float32), rows_of(weights, q * 3, 8, jnp.float32)
    cell = lax.broadcasted_iota(jnp.int32, (8, 128), 0).astype(jnp.float32)
    return [spread_rows(cell + 8.0 * k, cs, ws, jnp.float32) for k in range(TX // 8)]


def weights_y(corners, weights, q):
    cs, ws = rows_of(corners, q * 3 + 1, 8, jnp.float32), rows_of(weights, q * 3 + 1, 8, jnp.float32)
    cell = lax.broadcasted_iota(jnp.int32, (8, 128), 0).astype(jnp.float32)
    return spread_rows(cell, cs, ws, jnp.float32)


def weights_z(corners, weights, q, depth):
    cs, ws = rows_of(corners, q * 3 + 2, 16, jnp.bfloat16), rows_of(weights, q * 3 + 2, 16, jnp.bfloat16)
    cell = lax.broadcasted_iota(jnp.int32, (16, 128), 0).astype(jnp.float32)
    return [spread_rows((cell + 16.0 * k).astype(jnp.bfloat16), cs, ws, jnp.bfloat16) for k in range(depth // 16)]


def spread_kernel(tile_ref, recv_ref, velocity_ref, forced_ref, list_ref, acc_ref):
    depth = velocity_ref.shape[3]
    tiles_y = velocity_ref.shape[2] // TY
    slots = tile_ref.shape[0]
    total = list_slots(tile_ref, list_ref, slots)
    acc_ref[...] = jnp.zeros(acc_ref.shape, jnp.float32)

    def piece(slot):
        corners, weights = slot_weights(recv_ref, slot)
        device, rank = slot // 2, slot % 2
        kernel_xy, weighted = [], []
        for q in range(2):
            wx = weights_x(corners, weights, q)
            wy = weights_y(corners, weights, q)
            columns = [
                jnp.broadcast_to(wx[i // 8][i % 8 : i % 8 + 1, :], (8, 128)) * wy for i in range(TX)
            ]
            kernel_xy.append(jnp.concatenate(columns, axis=0).astype(jnp.bfloat16))
            wz = weights_z(corners, weights, q, depth)
            parts = []
            for c in range(3):
                row = device * ROWS + force_row(rank, q * 3 + c)
                force = jnp.broadcast_to(recv_ref[pl.ds(row, 1), :], (16, 128)).astype(jnp.bfloat16)
                parts += [w * force for w in wz]
            weighted.append(jnp.concatenate(parts, axis=0))
        a = jnp.concatenate(kernel_xy, axis=1)
        b = jnp.concatenate(weighted, axis=1)
        return lax.dot_general(a, b, (((1,), (1,)), ((), ())), preferred_element_type=jnp.float32)

    def add(tile, out):
        x0 = (tile // tiles_y) * TX
        y0 = pl.multiple_of((tile % tiles_y) * TY, TY)
        for c in range(3):
            block = out[:, c * depth : (c + 1) * depth].reshape(TX, TY, depth)
            here = (c, pl.ds(x0, TX), pl.ds(y0, TY), slice(None))
            acc_ref[here] = acc_ref[here] + block

    def pair(n, carry):
        first, second = list_ref[2 * n], list_ref[2 * n + 1]
        out0, out1 = piece(first), piece(second)
        add(tile_ref[first], out0)

        @pl.when(2 * n + 1 < total)
        def _():
            add(tile_ref[second], out1)

        return carry

    lax.fori_loop(0, (total + 1) // 2, pair, 0)
    forced_ref[...] = velocity_ref[...] + time_step * acc_ref[...]


def spread(tile, recv, velocity):
    smem = pl.BlockSpec(memory_space=pltpu.SMEM)
    vmem = pl.BlockSpec(memory_space=pltpu.VMEM)
    return pl.pallas_call(
        spread_kernel,
        out_shape=jax.ShapeDtypeStruct(velocity.shape, jnp.float32),
        in_specs=[smem, vmem, vmem],
        out_specs=vmem,
        scratch_shapes=[
            pltpu.SMEM((tile.shape[0] + 8,), jnp.int32),
            pltpu.VMEM(velocity.shape, jnp.float32),
        ],
        compiler_params=pltpu.CompilerParams(vmem_limit_bytes=40 << 20),
        name="spread",
    )(tile, recv, velocity)


def sweep_kernel(tile_ref, recv_ref, forced_ref, xlo_ref, xhi_ref, ylo_ref, yhi_ref, next_ref, reply_ref, list_ref, pad_ref, tiled_ref):
    _, size_x, size_y, depth = forced_ref.shape
    tiles_y = size_y // TY
    slots = tile_ref.shape[0]
    total = list_slots(tile_ref, list_ref, slots)
    pad_ref[:, 1 : size_x + 1, 8 : size_y + 8, :] = forced_ref[...]
    pad_ref[:, 0, 8 : size_y + 8, :] = xlo_ref[...]
    pad_ref[:, size_x + 1, 8 : size_y + 8, :] = xhi_ref[...]
    pad_ref[:, 1 : size_x + 1, 7, :] = ylo_ref[...]
    pad_ref[:, 1 : size_x + 1, size_y + 8, :] = yhi_ref[...]
    lane = lax.broadcasted_iota(jnp.int32, (TY, depth), 1)
    first_lane, last_lane = lane == 0, lane == depth - 1

    def column(x2, carry):
        for ty in range(tiles_y):
            y0 = 8 + ty * TY
            halves = [[], [], []]
            for dx in range(2):
                x = x2 * 2 + dx + 1
                centre = [pad_ref[c, x, y0 : y0 + TY, :] for c in range(3)]
                for c in range(3):
                    plus_x = pad_ref[c, x + 1, y0 : y0 + TY, :]
                    minus_x = pad_ref[c, x - 1, y0 : y0 + TY, :]
                    plus_y = pad_ref[c, x, y0 + 1 : y0 + TY + 1, :]
                    minus_y = pad_ref[c, x, y0 - 1 : y0 + TY - 1, :]
                    plus_z = jnp.where(last_lane, 0.0, pltpu.roll(centre[c], depth - 1, 1))
                    minus_z = jnp.where(first_lane, 0.0, pltpu.roll(centre[c], 1, 1))
                    laplace = plus_x + minus_x + plus_y + minus_y + plus_z + minus_z - 6.0 * centre[c]
                    advect = (
                        centre[0] * (plus_x - minus_x)
                        + centre[1] * (plus_y - minus_y)
                        + centre[2] * (plus_z - minus_z)
                    ) * 0.5
                    value = centre[c] + time_step * (viscosity * laplace - advect)
                    next_ref[c, x - 1, ty * TY : (ty + 1) * TY, :] = value
                    halves[c].append(value)
            tile = (x2 // (TX // 2)) * tiles_y + ty
            for c in range(3):
                row = pl.multiple_of((tile * 3 + c) * (TX * TY) + (x2 % (TX // 2)) * 16, 16)
                tiled_ref[pl.ds(row, 16), :] = jnp.concatenate(halves[c], axis=0).astype(jnp.bfloat16)
        return carry

    lax.fori_loop(0, size_x // 2, column, 0)

    def fetch(slot):
        corners, weights = slot_weights(recv_ref, slot)
        tile = tile_ref[slot]
        wz = jnp.concatenate(
            [jnp.concatenate(weights_z(corners, weights, q, depth), axis=0) for q in range(2)], axis=1
        )
        row = pl.multiple_of(tile * (3 * TX * TY), 16)
        field = tiled_ref[pl.ds(row, 3 * TX * TY), :]
        return corners, weights, lax.dot_general(
            field, wz, (((1,), (0,)), ((), ())), preferred_element_type=jnp.float32
        )

    def finish(slot, corners, weights, along):
        for q in range(2):
            wx = weights_x(corners, weights, q)
            wy = weights_y(corners, weights, q)
            wide = [jnp.broadcast_to(wx[i // 8][i % 8 : i % 8 + 1, :], (8, 128)) for i in range(TX)]
            for c in range(3):
                total_c = None
                for i in range(TX):
                    row = c * TX * TY + i * TY
                    term = wide[i] * along[row : row + TY, q * 128 : (q + 1) * 128]
                    total_c = term if total_c is None else total_c + term
                result = jnp.sum(total_c * wy, axis=0, keepdims=True)
                reply_ref[pl.ds(slot * 8 + q * 3 + c, 1), :] = result

    def pair(n, carry):
        first, second = list_ref[2 * n], list_ref[2 * n + 1]
        got0, got1 = fetch(first), fetch(second)
        finish(first, *got0)
        finish(second, *got1)
        return carry

    lax.fori_loop(0, (total + 1) // 2, pair, 0)


def sweep(tile, recv, forced, xlo, xhi, ylo, yhi):
    smem = pl.BlockSpec(memory_space=pltpu.SMEM)
    vmem = pl.BlockSpec(memory_space=pltpu.VMEM)
    _, size_x, size_y, depth = forced.shape
    slots = tile.shape[0]
    return pl.pallas_call(
        sweep_kernel,
        out_shape=(
            jax.ShapeDtypeStruct(forced.shape, jnp.float32),
            jax.ShapeDtypeStruct((slots * 8, 128), jnp.float32),
        ),
        in_specs=[smem] + [vmem] * 6,
        out_specs=(vmem, vmem),
        scratch_shapes=[
            pltpu.SMEM((slots + 8,), jnp.int32),
            pltpu.VMEM((3, size_x + 2, size_y + 16, depth), jnp.float32),
            pltpu.VMEM((3 * size_x * size_y, depth), jnp.bfloat16),
        ],
        compiler_params=pltpu.CompilerParams(vmem_limit_bytes=40 << 20),
        name="sweep",
    )(tile, recv, forced, xlo, xhi, ylo, yhi)


def gather_kernel(slot_ref, back_ref, out_ref):
    blocks = out_ref.shape[1]

    def take(group, carry):
        b0 = pl.multiple_of(group * 8, 8)
        starts = [slot_ref[b0 + j] * 8 for j in range(8)]
        for q in range(2):
            for c in range(3):
                rows = [back_ref[pl.ds(start + q * 3 + c, 1), :] for start in starts]
                out_ref[c, pl.ds(b0, 8), q * 128 : (q + 1) * 128] = jnp.concatenate(rows, axis=0)
        return carry

    lax.fori_loop(0, blocks // 8, take, 0)


def gather(slot, back):
    smem = pl.BlockSpec(memory_space=pltpu.SMEM)
    vmem = pl.BlockSpec(memory_space=pltpu.VMEM)
    return pl.pallas_call(
        gather_kernel,
        out_shape=jax.ShapeDtypeStruct((3, slot.shape[0], 256), jnp.float32),
        in_specs=[smem, vmem],
        out_specs=vmem,
        name="gather",
    )(slot, back)


def neighbour(value, axis, step):
    count = lax.axis_size(axis)
    return lax.ppermute(value, axis, [(i, i + step) for i in range(count) if 0 <= i + step < count])


def exchange(rows, devices):
    shaped = rows.reshape(devices, rows.shape[0] // devices, 128)
    return lax.all_to_all(shaped, AXES, split_axis=0, concat_axis=0, tiled=True)


def body(velocity, forces, offsets, base_x, base_y, base_z, home_device, home_tile):
    devices = lax.axis_size("gx") * lax.axis_size("gy")
    send, slot = pack(
        home_device[:, 0],
        home_tile,
        jnp.transpose(forces, (1, 0, 2)),
        jnp.transpose(offsets, (1, 0, 2)),
        base_x,
        base_y,
        base_z,
        devices,
    )
    recv = exchange(send, devices)
    tile = recv[:, 14:16, 0].astype(jnp.int32).reshape(-1)
    recv = recv.reshape(devices * ROWS, 128)
    forced = spread(tile, recv, velocity)
    xlo = neighbour(forced[:, -1], "gx", 1)
    xhi = neighbour(forced[:, 0], "gx", -1)
    ylo = neighbour(forced[:, :, -1], "gy", 1)
    yhi = neighbour(forced[:, :, 0], "gy", -1)
    velocity_next, reply = sweep(tile, recv, forced, xlo, xhi, ylo, yhi)
    back = exchange(reply, devices).reshape(-1, 128)
    fibre = gather(slot, back)
    return velocity_next, jnp.transpose(fibre, (1, 0, 2))


def solution(mesh):
    return jax.shard_map(
        body,
        mesh=mesh,
        in_specs=(
            P(None, "gx", "gy", None),
            P(AXES, None, None),
            P(AXES, None, None),
            P(AXES, None),
            P(AXES, None),
            P(AXES, None),
            P(AXES, None),
            P(AXES),
        ),
        out_specs=(P(None, "gx", "gy", None), P(AXES, None, None)),
        check_vma=False,
    )
```

time: 520 us -> 187 us (0.36)
  matrix products: 144 us -> 0 us
  other arithmetic: 135 us -> 2.23 us
  local copies, waits for them, and re-layouts: 132 us -> 2.12 us
  blocking collectives: 0 us -> 96.3 us
  Pallas kernels: 0 us -> 51.1 us
  waiting for transfers between devices: 51.5 us -> 0.86 us
  starting transfers between devices: 48.5 us -> 33.3 us
    dot_general x48 -> x0, matrix products: 144 us -> none  [the longest x16 111 us: spread_group(): jnp.einsum('gt,gab->tab', select, pieces, precision=lax.Precision.HIGHEST)]
    all_to_all x0 -> x2, blocking collectives: none -> 96.3 us  [exchange(): return lax.all_to_all(shaped, AXES, split_axis=0, concat_axis=0, tiled=True)]
    add x129 -> x0, other arithmetic: 63.6 us -> none  [the longest x96 52.7 us: dense_factor(): running + jnp.where(cell_ids == corner[..., None] + shift_amount, weight[...]
    squeeze x64 -> x1, local copies, waits for them, and re-layouts: 54.6 us -> 0.02 us  [body(): xhi = neighbour(forced[:, 0], 'gx', -1)]
    pallas_call x0 -> x4, Pallas kernels: none -> 51.1 us  [the longest x1 23.1 us: sweep(): pl.pallas_call(sweep_kernel, out_shape=(jax.ShapeDtypeStruct(forced.shape...]
    all_to_all x4 -> x0, waiting for transfers between devices: 49.3 us -> none  [the longest x1 27.6 us: body(): lax.all_to_all(send_float, ('gx', 'gy'), split_axis=0, concat_axis=0, til...]
    all_to_all x4 -> x0, starting transfers between devices: 36.7 us -> none  [the longest x1 11.5 us: body(): lax.all_to_all(send_tile, ('gx', 'gy'), split_axis=0, concat_axis=0, tile...]
    scatter x3 -> x0, local copies, waits for them, and re-layouts: 28 us -> none  [the longest x1 13.7 us: body(): jnp.zeros((slot_count, 6, points), jnp.float32).at[slot_index].set(payload)]
  transfers between devices with their start and end apart: 8 -> 4, of which waited for: 6 -> 1; matrix products, arithmetic and copies ran while one was open for 7% -> 0% of each run, Pallas kernels for 0% -> 0%
where the time goes in v1:
time: 187 us
  blocking collectives  96.3 us (51%)
  Pallas kernels  51.1 us (27%)
  starting transfers between devices  33.3 us (18%)
  other arithmetic  2.23 us (1%)
  local copies, waits for them, and re-layouts  2.12 us (1%)
    all_to_all x2, blocking collectives, exchange(): return lax.all_to_all(shaped, AXES, split_axis=0, concat_axis=0, tiled=True)  96.3 us
    ppermute x4, starting transfers between devices, neighbour(): lax.ppermute(value, axis, [(i, i + step) for i in range(count) if 0 <= i...  33.3 us
    pallas_call x1, Pallas kernels, sweep(): pl.pallas_call(sweep_kernel, out_shape=(jax.ShapeDtypeStruct(forced.shape...  23.1 us
    pallas_call x1, Pallas kernels, spread(): pl.pallas_call(spread_kernel, out_shape=jax.ShapeDtypeStruct(velocity.sha...  20.6 us
    pallas_call x1, Pallas kernels, pack(): pl.pallas_call(pack_kernel, out_shape=(jax.ShapeDtypeStruct((devices * RO...  5.11 us
  transfers between devices with their start and end apart: 4, of which 1 were waited for; matrix products, arithmetic and copies ran while one was open for 0% of the time, Pallas kernels for 0%

profile of v1, /device:TPU:1, one launch (start us, length us, event | category | flops | bytes accessed | tf_op | source)
XLA Modules:
  0.0 186.6 jit_solution(3343679992488797004)
XLA Ops:
  0.6 5.1 %pack.1 = (f32[5120,128]{1,0:T(8,128)}, s32[128]{0:T(128)}) custom-call(s32[128]{0:T(128)} %bitcast.32, s32[128]{0:T(128)} %tile_ref.1, f32[3,128,256]{2,1,0:T(8,128)} %bitcast.27, f32[3,128,256]{2,1,0:T(8,128)} %bitcast.28, s32[128,256]{1,0:T(8,128)} %bx_ref.1, s32[128,256]{1,0:T(8,128)} %by_ref.1, s32[128,256]{1,0:T(8,128)} %bz_ref.1), custom_call_target="tpu_custom_call" | custom-call | tf_op jit(solution)/shard_map/pack/pallas_call | solution.py:65
  5.8 47.4 %all_to_all.10 = f32[128,40,128]{2,1,0:T(8,128)S(1)} all-to-all(f32[128,40,128]{2,1,0:T(8,128)} %bitcast.26), channel_id=1, replica_groups=mesh['gx'=16,'gy'=8] {'gx','gy'}, dimensions={0} | all-to-all | bytes 5242880 | tf_op jit(solution)/shard_map/all_to_all | solution.py:341
  53.2 2.2 %fusion = s32[128,2]{1,0:T(8,128)S(1)} fusion(f32[128,40,128]{2,1,0:T(8,128)S(1)} %all_to_all.10), kind=kLoop, calls=%fused_computation.1 | loop fusion | flops 256 | bytes 2048 | tf_op jit(solution)/shard_map/convert_element_type | solution.py:357
  55.4 0.1 convert_element_type.8.tile_ref
  55.6 0.0 copy-start
  55.6 1.9 %copy-done = f32[3,32,64,128]{3,2,1,0:T(8,128)S(1)} copy-done((f32[3,32,64,128]{3,2,1,0:T(8,128)S(1)}, f32[3,32,64,128]{3,2,1,0:T(8,128)}, u32[]{:S(2)}) %copy-start) | copy-done | bytes 3145752
  57.5 20.6 %spread.1.forced_ref = f32[3,32,64,128]{3,2,1,0:T(8,128)S(1)} custom-call(s32[256]{0:T(256)S(1)} %convert_element_type.8.tile_ref, f32[5120,128]{1,0:T(8,128)S(1)} %bitcast.22, f32[3,32,64,128]{3,2,1,0:T(8,128)S(1)} %copy-done), custom_call_target="tpu_custom_call" | custom-call | tf_op jit(solution)/shard_map/spread/pallas_call | solution.py:190
  78.1 1.3 collective-permute-start.1
  79.4 4.0 %collective-permute-start = (f32[3,64,128]{2,1,0:T(8,128)S(1)}, f32[3,64,128]{2,1,0:T(8,128)S(1)}, u32[]{:S(2)}, u32[]{:S(2)}) collective-permute-start(f32[3,64,128]{2,1,0:T(8,128)S(1)} %get-tuple-element.13), channel_id=1, source_target_pairs={{0,8},{8,16},{16,24},{24,32},{32,40},{40,48},{48,56},{56,64},{64,7... | collective-permute-start | bytes 294920 | tf_op jit(solution)/shard_map/ppermute | solution.py:336
  83.4 0.1 fusion.1
  83.4 3.2 %collective-permute-start.2 = (f32[3,32,128]{2,1,0:T(8,128)S(1)}, f32[3,32,128]{2,1,0:T(8,128)S(1)}, u32[]{:S(2)}, u32[]{:S(2)}) collective-permute-start(f32[3,32,128]{2,1,0:T(8,128)S(1)} %bitcast.31), channel_id=1, source_target_pairs={{0,1},{1,2},{2,3},{3,4},{4,5},{5,6},{6,7},{8,9},{9,10},{10,11},{11... | collective-permute-start | bytes 147464 | tf_op jit(solution)/shard_map/ppermute | solution.py:336
  86.6 24.8 %collective-permute-start.3 = (f32[3,32,128]{2,1,0:T(8,128)S(1)}, f32[3,32,128]{2,1,0:T(8,128)S(1)}, u32[]{:S(2)}, u32[]{:S(2)}) collective-permute-start(f32[3,32,128]{2,1,0:T(8,128)S(1)} %bitcast.30), channel_id=1, source_target_pairs={{1,0},{2,1},{3,2},{4,3},{5,4},{6,5},{7,6},{9,8},{10,9},{11,10},{12... | collective-permute-start | bytes 147464 | tf_op jit(solution)/shard_map/ppermute | solution.py:336
  111.4 0.0 collective-permute-done.2.ylo_ref
  111.4 0.8 collective-permute-done.3.yhi_ref
  112.3 0.0 collective-permute-done.1.xhi_ref
  112.3 0.0 collective-permute-done.xlo_ref
  112.3 23.1 %sweep.1 = (f32[3,32,64,128]{3,2,1,0:T(8,128)}, f32[2048,128]{1,0:T(8,128)S(1)}) custom-call(s32[256]{0:T(256)S(1)} %convert_element_type.8.tile_ref, f32[5120,128]{1,0:T(8,128)S(1)} %bitcast.23, f32[3,32,64,128]{3,2,1,0:T(8,128)S(1)} %spread.1.forced_ref, f32[3,64,128]{2,1,0:T(8,128)S(1)} %collective-permute-done.xlo_ref, ...), custom_call_target="tpu_custom_call" | custom-call | tf_op jit(solution)/shard_map/sweep/pallas_call | solution.py:289
  135.3 48.9 %all_to_all.11 = f32[128,16,128]{2,1,0:T(8,128)} all-to-all(f32[128,16,128]{2,1,0:T(8,128)S(1)} %bitcast.24), channel_id=1, replica_groups=mesh['gx'=16,'gy'=8] {'gx','gy'}, dimensions={0} | all-to-all | bytes 2097152 | tf_op jit(solution)/shard_map/all_to_all | solution.py:341
  184.2 2.3 %gather.1 = f32[3,128,256]{2,1,0:T(8,128)} custom-call(s32[128]{0:T(128)} %get-tuple-element.8.slot_ref, f32[2048,128]{1,0:T(8,128)} %bitcast.25), custom_call_target="tpu_custom_call" | custom-call | tf_op jit(solution)/shard_map/gather/pallas_call | solution.py:325
  (1 shorter events, 0.0 us)
Async XLA Ops:
  55.6 1.9 %copy-start = (f32[3,32,64,128]{3,2,1,0:T(8,128)S(1)}, f32[3,32,64,128]{3,2,1,0:T(8,128)}, u32[]{:S(2)}) copy-start(f32[3,32,64,128]{3,2,1,0:T(8,128)} %velocity_ref.1) | copy-start | bytes 9437188
  78.1 34.2 %collective-permute-start.1 = (f32[3,64,128]{2,1,0:T(8,128)S(1)}, f32[3,64,128]{2,1,0:T(8,128)S(1)}, u32[]{:S(2)}, u32[]{:S(2)}) collective-permute-start(f32[3,64,128]{2,1,0:T(8,128)S(1)} %get-tuple-element.12), channel_id=1, source_target_pairs={{8,0},{16,8},{24,16},{32,24},{40,32},{48,40},{56,48},{64,56},{72,6... | collective-permute-start | bytes 294920 | tf_op jit(solution)/shard_map/ppermute | solution.py:336
  79.4 32.9 %collective-permute-start = (f32[3,64,128]{2,1,0:T(8,128)S(1)}, f32[3,64,128]{2,1,0:T(8,128)S(1)}, u32[]{:S(2)}, u32[]{:S(2)}) collective-permute-start(f32[3,64,128]{2,1,0:T(8,128)S(1)} %get-tuple-element.13), channel_id=1, source_target_pairs={{0,8},{8,16},{16,24},{24,32},{32,40},{40,48},{48,56},{56,64},{64,7... | collective-permute-start | bytes 294920 | tf_op jit(solution)/shard_map/ppermute | solution.py:336
  83.4 28.0 %collective-permute-start.2 = (f32[3,32,128]{2,1,0:T(8,128)S(1)}, f32[3,32,128]{2,1,0:T(8,128)S(1)}, u32[]{:S(2)}, u32[]{:S(2)}) collective-permute-start(f32[3,32,128]{2,1,0:T(8,128)S(1)} %bitcast.31), channel_id=1, source_target_pairs={{0,1},{1,2},{2,3},{3,4},{4,5},{5,6},{6,7},{8,9},{9,10},{10,11},{11... | collective-permute-start | bytes 147464 | tf_op jit(solution)/shard_map/ppermute | solution.py:336
  86.6 25.6 %collective-permute-start.3 = (f32[3,32,128]{2,1,0:T(8,128)S(1)}, f32[3,32,128]{2,1,0:T(8,128)S(1)}, u32[]{:S(2)}, u32[]{:S(2)}) collective-permute-start(f32[3,32,128]{2,1,0:T(8,128)S(1)} %bitcast.30), channel_id=1, source_target_pairs={{1,0},{2,1},{3,2},{4,3},{5,4},{6,5},{7,6},{9,8},{10,9},{11,10},{12... | collective-permute-start | bytes 147464 | tf_op jit(solution)/shard_map/ppermute | solution.py:336
